TPU v7x, 1024 devices: a whole 8x8x8 slice. The times are simulated.
1024 devices in a mesh: row: 16 (over z, core), col: 64 (over y, x).
Axes of the slice: x: 8, y: 8, z: 8, core: 2. Of those that a mesh axis runs over, the one named last changes fastest.
Arguments:
- gate_pre: bfloat16 [4096, 16384], P('row', 'col'), may hold values from -8 to 8
- up_pre: bfloat16 [4096, 16384], P('row', 'col'), may hold values from -6 to 6
- down_t: bfloat16 [4096, 16384], P('row', 'col'), may hold values from -0.09375 to 0.09375
- grad_out: bfloat16 [4096, 4096], P('row', 'col'), may hold values from -16 to 16
Outputs:
- gate_grad: bfloat16 [4096, 16384], P('row', 'col')
- up_grad: bfloat16 [4096, 16384], P('row', 'col')
- weight_grad: bfloat16 [4096, 16384], P('row', 'col')
All inputs are finite; a program needn't handle non-finite values.
Results may differ from a plain program's by a relative error of at most 0.0049.
Values may be sent and summed in bfloat16 or wider, within the bound.
A program may use at most 32 MiB of HBM per device.

v0:
```python
import jax
import jax.numpy as jnp
from jax import lax
from jax.sharding import PartitionSpec as P


def panel_adder(grad_full, piece):
    return jnp.dot(grad_full, piece, preferred_element_type=jnp.float32)


def per_device(gate_pre, up_pre, down_t, grad_out):
    tok_rows = grad_out.shape[0]
    norm_scale = (tok_rows * lax.axis_size("row")) ** (-0.5)
    gate_value = gate_pre.astype(jnp.float32)
    up_value = up_pre.astype(jnp.float32)
    gate_sigmoid = jax.nn.sigmoid(gate_value)
    activated = gate_value * gate_sigmoid
    hidden = (activated * up_value).astype(jnp.bfloat16)
    grad_full = lax.all_gather(grad_out, "col", axis=1, tiled=True)
    hidden_grad = panel_adder(grad_full, lax.all_gather(down_t, "row", axis=0, tiled=True))
    weight_sum = lax.psum_scatter(
        lax.dot_general(
            grad_full, hidden, (((0,), (0,)), ((), ())), preferred_element_type=jnp.float32
        ),
        "row",
        scatter_dimension=0,
        tiled=True,
    )
    weight_grad = (weight_sum * norm_scale).astype(jnp.bfloat16)
    up_grad = (hidden_grad * activated).astype(jnp.bfloat16)
    slope = gate_sigmoid * (1.0 + gate_value * (1.0 - gate_sigmoid))
    gate_grad = (hidden_grad * up_value * slope).astype(jnp.bfloat16)
    return (gate_grad, up_grad, weight_grad)


def solution(mesh):
    in_specs = (P("row", "col"), P("row", "col"), P("row", "col"), P("row", "col"))
    out_specs = (P("row", "col"), P("row", "col"), P("row", "col"))
    return jax.shard_map(
        per_device, mesh=mesh, in_specs=in_specs, out_specs=out_specs, check_vma=False
    )
```

profile of v0, /device:TPU:1, one launch (start us, length us, event | category | flops | bytes accessed | tf_op | source)
XLA Modules:
  0.0 237.6 jit_solution(10917887100531376375)
XLA Ops:
  7.2 0.0 all-gather.3.cloned.1.call-start
  7.2 0.7 all-gather.3.cloned.1.call-update
  7.9 0.0 all-gather.5.cloned.1.call-start
  7.9 0.7 all-gather.5.cloned.1.call-update
  8.6 0.0 reduce-scatter.2.cloned.1.call-start
  8.7 100.1 %all-gather.3.cloned.1.call-done = bf16[256,4096]{0,1:T(8,128)(2,1)} async-done(((bf16[256,64]{0,1:T(8,128)(2,1)}), bf16[256,4096]{0,1:T(8,128)(2,1)}) %all-gather.3.cloned.1.call-update) | async-done | bytes 2097168 | tf_op jit(solution)/shard_map/all_gather | solution.py:19
  108.8 4.5 %convolution_bitcast_fusion = f32[4096,256]{0,1:T(8,128)} fusion(bf16[256,4096]{0,1:T(8,128)(2,1)} %all-gather.3.cloned.1.call-done, bf16[256,256]{1,0:T(8,128)(2,1)} %param.5, bf16[256,256]{1,0:T(8,128)(2,1)} %param.4), kind=kOutput, calls=%fused_computation | convolution fusion | flops 537395200 | bytes 6553600 | tf_op jit(solution)/shard_map/dot_general | solution.py:22
  113.3 0.0 copy-start
  113.3 0.0 copy-start.1
  113.3 0.0 copy-start.2
  113.3 0.0 reduce-scatter.2.cloned.1.call-update
  113.3 47.9 %all-gather.5.cloned.1.call-done = bf16[4096,256]{1,0:T(8,128)(2,1)} async-done(((bf16[256,256]{1,0:T(8,128)(2,1)}), bf16[4096,256]{1,0:T(8,128)(2,1)}) %all-gather.5.cloned.1.call-update) | async-done | bytes 2097168 | tf_op jit(solution)/shard_map/all_gather | solution.py:20
  161.2 0.0 copy-done
  161.2 0.0 copy-done.1
  161.2 0.0 copy-done.2
  161.2 3.1 %multiply_convert_fusion.1 = (bf16[256,256]{1,0:T(8,128)(2,1)}, bf16[256,256]{1,0:T(8,128)(2,1)}) fusion(bf16[256,256]{1,0:T(8,128)(2,1)S(1)} %copy-done.1, bf16[256,256]{1,0:T(8,128)(2,1)S(1)} %copy-done.2, bf16[256,4096]{0,1:T(8,128)(2,1)S(1)} %copy-done, bf16[4096,256]{1,0:T(8,128)(2,1)} %all-gather.5.cloned.1.call-done), kind=kOutput, calls=%fused_computation.15 | convolution fusion | flops 537853952 | bytes 4718592 | tf_op jit(solution)/shard_map/dot_general | solution.py:8
  164.3 65.0 %reduce-scatter.2.cloned.1.call-done = f32[256,256]{0,1:T(8,128)} async-done(((f32[4096,256]{0,1:T(8,128)}), f32[256,256]{0,1:T(8,128)}) %reduce-scatter.2.cloned.1.call-update) | async-done | bytes 262160 | tf_op jit(solution)/shard_map/reduce_scatter | solution.py:21
  229.3 1.0 multiply_convert_fusion
  230.3 0.8 copy.7
Async XLA Ops:
  7.2 101.6 %all-gather.3.cloned.1.call-start = ((), (), s32[]{:S(2)}) async-start(), calls=%async_computation.1 | async-start | bytes 2129920 | tf_op jit(solution)/shard_map/all_gather | solution.py:19
  7.9 153.3 %all-gather.5.cloned.1.call-start = ((), (), s32[]{:S(2)}) async-start(), calls=%async_computation.2 | async-start | bytes 2228224 | tf_op jit(solution)/shard_map/all_gather | solution.py:20
  8.6 220.7 %reduce-scatter.2.cloned.1.call-start = ((), (), s32[]{:S(2)}) async-start(), calls=%async_computation.3 | async-start | bytes 4456448 | tf_op jit(solution)/shard_map/reduce_scatter | solution.py:21
  113.3 48.0 %copy-start = (bf16[256,4096]{0,1:T(8,128)(2,1)S(1)}, bf16[256,4096]{0,1:T(8,128)(2,1)}, u32[]{:S(2)}) copy-start(bf16[256,4096]{0,1:T(8,128)(2,1)} %all-gather.3.cloned.1.call-done) | copy-start | bytes 6291460
  113.3 48.0 %copy-start.1 = (bf16[256,256]{1,0:T(8,128)(2,1)S(1)}, bf16[256,256]{1,0:T(8,128)(2,1)}, u32[]{:S(2)}) copy-start(bf16[256,256]{1,0:T(8,128)(2,1)} %param.4) | copy-start | bytes 393220
  113.3 48.0 %copy-start.2 = (bf16[256,256]{1,0:T(8,128)(2,1)S(1)}, bf16[256,256]{1,0:T(8,128)(2,1)}, u32[]{:S(2)}) copy-start(bf16[256,256]{1,0:T(8,128)(2,1)} %param.5) | copy-start | bytes 393220
Sparse Core Ops, SparseCore 0:
  12.2 96.5 all-gather.2
  111.5 49.6 all-gather.4
  164.7 64.6 reduce-scatter.1
where the time goes:
time: 240 us; the launch traced here: 238 us
  waiting for transfers between devices  214 us (89%)
  between operations  13.7 us (6%)
  matrix products  7.53 us (3%)
    all_gather x1, waiting for transfers between devices, per_device(): grad_full = lax.all_gather(grad_out, 'col', axis=1, tiled=True)  100 us
    reduce_scatter x1, waiting for transfers between devices, per_device(): lax.psum_scatter(lax.dot_general(grad_full, hidden, (((0,), (0,)), ((), (...  65 us
    all_gather x1, waiting for transfers between devices, per_device(): lax.all_gather(down_t, 'row', axis=0, tiled=True)  47.9 us
  transfers between devices with their start and end apart: 3, of which 3 were waited for; matrix products, arithmetic and copies ran while one was open for 3% of the time, Pallas kernels for 0%

commit v1 on v0

v1 whole, which is shorter than its diff:
```python
import jax
import jax.numpy as jnp
from jax import lax
from jax.experimental import pallas as pl
from jax.experimental.pallas import tpu as pltpu
from jax.sharding import PartitionSpec as P

N = 8
BF = jnp.bfloat16
F32 = jnp.float32


def md(v):
    return lax.rem(v + 2 * N, N)


def kernel(
    gate_ref,
    up_ref,
    down_ref,
    go_ref,
    ggrad_ref,
    ugrad_ref,
    wgrad_ref,
    gt,
    gp,
    wf,
    hid,
    act,
    ups,
    part,
    got,
    hg,
    a1,
    b1,
    a2r,
    a2l,
    b2r,
    b2l,
    pa,
    pb,
    wr,
    wl,
    wp,
    hp,
    rs,
    s1,
    s2,
    sp,
    sb,
    sw,
    swp,
    sh,
    srs,
):
    row, col = lax.axis_index("row"), lax.axis_index("col")
    z, c = lax.div(row, 2), lax.rem(row, 2)
    y, x = lax.div(col, N), lax.rem(col, N)
    cp = 1 - c

    def at_x(v):
        return {"row": row, "col": y * N + v}

    def at_y(v):
        return {"row": row, "col": v * N + x}

    def at_z(v):
        return {"row": v * 2 + c, "col": col}

    partner = {"row": z * 2 + cp, "col": col}

    def send(ref, dst, ssem, rsem, dev):
        pltpu.make_async_remote_copy(
            src_ref=ref, dst_ref=dst, send_sem=ssem, recv_sem=rsem, device_id=dev
        ).start()

    def arrived(ref, sem):
        pltpu.make_async_copy(ref, ref, sem).wait()

    barrier = pltpu.get_barrier_semaphore()
    for k in range(1, N):
        pl.semaphore_signal(barrier, inc=1, device_id=at_x(md(x + k)))
        pl.semaphore_signal(barrier, inc=1, device_id=at_y(md(y + k)))
        pl.semaphore_signal(barrier, inc=1, device_id=at_z(md(z + k)))
    pl.semaphore_signal(barrier, inc=1, device_id=partner)

    eye = (
        lax.broadcasted_iota(jnp.int32, (64, 64), 0)
        == lax.broadcasted_iota(jnp.int32, (64, 64), 1)
    ).astype(BF)
    gt[y, x] = lax.dot_general(
        eye, go_ref[...], (((1,), (1,)), ((), ())), preferred_element_type=F32
    ).astype(BF)
    wf[z, c] = down_ref[...]

    pl.semaphore_wait(barrier, 3 * (N - 1) + 1)

    own_a = gt.at[y, x, pl.ds(0, 32)]
    own_b = gt.at[y, x, pl.ds(32, 32)]
    for k in (4, 3, 5, 2, 6, 1, 7):
        send(own_a, own_a, s1, a1.at[k], at_x(md(x + k)))
        send(own_b, own_b, s1, b1.at[k], at_y(md(y + k)))

    def w_ref(v, half=None):
        return wf.at[v, c] if half is None else wf.at[v, c, pl.ds(128 * half, 128)]

    def w_step(s):
        right = w_ref(md(z - s), 0 if s == 3 else None)
        left = w_ref(md(z + s), 1 if s == 3 else None)
        if s > 0:
            full_r, full_l = w_ref(md(z - s)), w_ref(md(z + s))
            arrived(full_r, wr.at[s - 1])
            send(right, right, sw, wr.at[s], at_z(md(z + 1)))
            arrived(full_l, wl.at[s - 1])
            send(left, left, sw, wl.at[s], at_z(md(z - 1)))
            send(full_r, full_r, swp, wp, partner)
            send(full_l, full_l, swp, wp, partner)
        else:
            send(right, right, sw, wr.at[s], at_z(md(z + 1)))
            send(left, left, sw, wl.at[s], at_z(md(z - 1)))
            send(right, right, swp, wp, partner)

    w_step(0)

    gate = gate_ref[...].astype(F32)
    up = up_ref[...].astype(F32)
    sig = jax.nn.sigmoid(gate)
    activated = gate * sig
    act[...] = activated
    ups[...] = up * (sig * (1.0 + gate * (1.0 - sig)))
    hid[0] = (activated * up).astype(BF)
    send(hid.at[0], hid.at[1], sh, hp, partner)

    def a_ref(v, h):
        return gt.at[v, pl.ds(4 * h, 4), pl.ds(0, 32)]

    def b_ref(v, h):
        return gt.at[pl.ds(4 * h, 4), v, pl.ds(32, 32)]

    def ring(s, h):
        if not (s == 3 and h == 1):
            ra, rb = a_ref(md(y - s), h), b_ref(md(x - s), h)
            if s > 0:
                arrived(ra, a2r.at[s - 1, h])
            send(ra, ra, s2, a2r.at[s, h], at_y(md(y + 1)))
            if s > 0:
                arrived(rb, b2r.at[s - 1, h])
            send(rb, rb, s2, b2r.at[s, h], at_x(md(x + 1)))
        elif s == 3:
            ra, rb = a_ref(md(y - s), h), b_ref(md(x - s), h)
            arrived(ra, a2r.at[s - 1, h])
            arrived(rb, b2r.at[s - 1, h])
        la, lb = a_ref(md(y + s), h), b_ref(md(x + s), h)
        if s > 0:
            arrived(la, a2l.at[s - 1, h])
        if not (s == 3 and h == 0):
            send(la, la, s2, a2l.at[s, h], at_y(md(y - 1)))
        if s > 0:
            arrived(lb, b2l.at[s - 1, h])
        if not (s == 3 and h == 0):
            send(lb, lb, s2, b2l.at[s, h], at_x(md(x - 1)))

    def share(j, yv, xv):
        theirs = gt.at[yv, pl.ds(4 * cp, 4), pl.ds(0, 32)]
        send(theirs, gp.at[yv, slice(None), pl.ds(0, 32)], sp, pa.at[j], partner)

        @pl.when(lax.div(xv, 4) == cp)
        def _():
            send(
                gt.at[slice(None), xv, pl.ds(32, 32)],
                gp.at[slice(None), lax.rem(xv, 4), pl.ds(32, 32)],
                sb,
                pb.at[j],
                partner,
            )

    def reduce(j, yv, xv):
        mine = gp.at[yv, slice(None), pl.ds(0, 32)]
        arrived(mine, pa.at[j])
        total = jnp.dot(
            gt[yv, pl.ds(4 * c, 4), pl.ds(0, 32)].reshape(128, 256),
            hid[0],
            preferred_element_type=F32,
        ) + jnp.dot(
            gp[yv, :, pl.ds(0, 32)].reshape(128, 256),
            hid[1],
            preferred_element_type=F32,
        )
        part[yv, :, pl.ds(0, 32)] = total.astype(BF).reshape(4, 32, 256)
        away = md(yv - z)

        @pl.when(away != 0)
        def _():
            send(
                part.at[yv, slice(None), pl.ds(0, 32)],
                got.at[away - 1, slice(None), pl.ds(0, 32)],
                srs,
                rs,
                at_z(yv),
            )

        @pl.when(lax.div(xv, 4) == c)
        def _():
            xi = lax.rem(xv, 4)
            arrived(gp.at[slice(None), xi, pl.ds(32, 32)], pb.at[j])
            total_b = jnp.dot(
                gt[:, xv, pl.ds(32, 32)].reshape(256, 256),
                hid[0],
                preferred_element_type=F32,
            ) + jnp.dot(
                gp[:, xi, pl.ds(32, 32)].reshape(256, 256),
                hid[1],
                preferred_element_type=F32,
            )
            part[:, xi, pl.ds(32, 32)] = total_b.astype(BF).reshape(N, 32, 256)
            for k in (4, 3, 5, 2, 6, 1, 7):
                send(
                    part.at[md(z + k), xi, pl.ds(32, 32)],
                    got.at[k - 1, xi, pl.ds(32, 32)],
                    srs,
                    rs,
                    at_z(md(z + k)),
                )

    for k in range(1, N):
        arrived(gt.at[y, md(x - k), pl.ds(0, 32)], a1.at[k])
        arrived(gt.at[md(y - k), x, pl.ds(32, 32)], b1.at[k])
    ring(0, 0)
    ring(0, 1)
    share(0, y, x)
    arrived(hid.at[1], hp)
    ring(1, 0)
    ring(1, 1)
    share(1, md(y - 1), md(x - 1))
    share(2, md(y + 1), md(x + 1))
    reduce(0, y, x)
    w_step(1)
    ring(2, 0)
    ring(2, 1)
    share(3, md(y - 2), md(x - 2))
    share(4, md(y + 2), md(x + 2))
    reduce(1, md(y - 1), md(x - 1))
    reduce(2, md(y + 1), md(x + 1))
    w_step(2)
    ring(3, 0)
    ring(3, 1)
    share(5, md(y - 3), md(x - 3))
    share(6, md(y + 3), md(x + 3))
    reduce(3, md(y - 2), md(x - 2))
    reduce(4, md(y + 2), md(x + 2))
    w_step(3)
    arrived(a_ref(md(y + 4), 0), a2r.at[3, 0])
    arrived(a_ref(md(y + 4), 1), a2l.at[3, 1])
    arrived(b_ref(md(x + 4), 0), b2r.at[3, 0])
    arrived(b_ref(md(x + 4), 1), b2l.at[3, 1])
    share(7, md(y + 4), md(x + 4))
    reduce(5, md(y - 3), md(x - 3))
    reduce(6, md(y + 3), md(x + 3))
    reduce(7, md(y + 4), md(x + 4))
    far = md(z + 4)
    arrived(w_ref(far, 0), wr.at[3])
    arrived(w_ref(far, 1), wl.at[3])
    send(w_ref(far), w_ref(far), swp, wp, partner)
    arrived(wf.at[slice(None), cp], wp)

    hg[...] = jnp.zeros_like(hg)

    @pl.loop(0, N)
    def _(v):
        both = gt[v].reshape(512, 256)
        hg[...] += lax.dot_general(
            both,
            wf[v].reshape(512, 256),
            (((0,), (0,)), ((), ())),
            preferred_element_type=F32,
        )

    ugrad_ref[...] = (hg[...] * act[...]).astype(BF)
    ggrad_ref[...] = (hg[...] * ups[...]).astype(BF)

    own = jnp.dot(
        gt[z, pl.ds(4 * c, 4)].reshape(256, 256), hid[0], preferred_element_type=F32
    ) + jnp.dot(gp[z].reshape(256, 256), hid[1], preferred_element_type=F32)

    arrived(gt.at[slice(0, 7), slice(0, 1)], s1)
    arrived(gt.at[slice(0, 7)], s2)
    arrived(gp.at[slice(None), slice(None), pl.ds(0, 32)], sp)
    arrived(gp.at[slice(None), slice(None), pl.ds(32, 32)], sb)
    arrived(wf.at[slice(0, 7), 0], sw)
    arrived(wf.at[slice(None), 0], swp)
    arrived(hid.at[0], sh)
    arrived(got, srs)
    arrived(got, rs)
    total = own
    for k in range(N - 1):
        total = total + got[k].reshape(256, 256).astype(F32)
    wgrad_ref[...] = (total * (1.0 / 64.0)).astype(BF)


def per_device(gate_pre, up_pre, down_t, grad_out):
    vmem = pl.BlockSpec(memory_space=pltpu.VMEM)
    block = jax.ShapeDtypeStruct((256, 256), BF)
    dma = pltpu.SemaphoreType.DMA
    return pl.pallas_call(
        kernel,
        out_shape=(block, block, block),
        in_specs=[vmem] * 4,
        out_specs=(vmem, vmem, vmem),
        scratch_shapes=[
            pltpu.VMEM((N, N, 64, 256), BF),
            pltpu.VMEM((N, 4, 64, 256), BF),
            pltpu.VMEM((N, 2, 256, 256), BF),
            pltpu.VMEM((2, 256, 256), BF),
            pltpu.VMEM((256, 256), F32),
            pltpu.VMEM((256, 256), F32),
            pltpu.VMEM((N, 4, 64, 256), BF),
            pltpu.VMEM((N - 1, 4, 64, 256), BF),
            pltpu.VMEM((256, 256), F32),
            dma((N,)),
            dma((N,)),
            dma((4, 2)),
            dma((4, 2)),
            dma((4, 2)),
            dma((4, 2)),
            dma((N,)),
            dma((N,)),
            dma((4,)),
            dma((4,)),
            dma,
            dma,
            dma,
            dma,
            dma,
            dma,
            dma,
            dma,
            dma,
            dma,
            dma,
        ],
        compiler_params=pltpu.CompilerParams(
            collective_id=0, has_side_effects=True, vmem_limit_bytes=40 << 20
        ),
    )(gate_pre, up_pre, down_t, grad_out)


def solution(mesh):
    spec = P("row", "col")
    return jax.shard_map(
        per_device,
        mesh=mesh,
        in_specs=(spec, spec, spec, spec),
        out_specs=(spec, spec, spec),
        check_vma=False,
    )
```

time: 240 us -> 77.7 us (0.32)
  the two profiles are of different devices: /device:TPU:1 before, /device:TPU:58 now
where the time goes in v1:
time: 77.7 us; the launch traced here: 77.4 us
  Pallas kernels  71.2 us (92%)
  local copies, waits for them, and re-layouts  5.55 us (7%)
    pallas_call x1, Pallas kernels, per_device(): pl.pallas_call(kernel, out_shape=(block, block, block), in_specs=[vmem] *...  71.2 us
    unnamed x10, local copies, waits for them, and re-layouts  5.55 us

profile of v1, /device:TPU:58, one launch (start us, length us, event | category | flops | bytes accessed | tf_op | source)
XLA Modules:
  0.0 77.4 jit_solution(17125769230640399808)
XLA Ops:
  0.6 0.9 %copy.7.go_ref = bf16[256,64]{1,0:T(8,128)(2,1)S(1)} copy(bf16[256,64]{0,1:T(8,128)(2,1)} %param.7) | data formatting | bytes 65536 | tf_op args[3]
  1.5 0.0 copy-start
  1.5 0.9 %copy-done = bf16[256,256]{1,0:T(8,128)(2,1)S(1)} copy-done((bf16[256,256]{1,0:T(8,128)(2,1)S(1)}, bf16[256,256]{1,0:T(8,128)(2,1)}, u32[]{:S(2)}) %copy-start) | copy-done | bytes 131096
  2.4 0.0 copy-start.1
  2.4 0.9 %copy-done.1 = bf16[256,256]{1,0:T(8,128)(2,1)S(1)} copy-done((bf16[256,256]{1,0:T(8,128)(2,1)S(1)}, bf16[256,256]{1,0:T(8,128)(2,1)}, u32[]{:S(2)}) %copy-start.1) | copy-done | bytes 131096
  3.3 0.0 copy-start.2
  3.3 0.9 %copy-done.2 = bf16[256,256]{1,0:T(8,128)(2,1)S(1)} copy-done((bf16[256,256]{1,0:T(8,128)(2,1)S(1)}, bf16[256,256]{1,0:T(8,128)(2,1)}, u32[]{:S(2)}) %copy-start.2) | copy-done | bytes 131096
  4.2 71.2 %shard_map.67 = (bf16[256,256]{1,0:T(8,128)(2,1)S(1)}, bf16[256,256]{1,0:T(8,128)(2,1)S(1)}, bf16[256,256]{1,0:T(8,128)(2,1)S(1)}) custom-call(bf16[256,256]{1,0:T(8,128)(2,1)S(1)} %copy-done, bf16[256,256]{1,0:T(8,128)(2,1)S(1)} %copy-done.1, bf16[256,256]{1,0:T(8,128)(2,1)S(1)} %copy-done.2, bf16[256,64]{1,0:T(8,128)(2,1)S(1)} %copy.7.go_ref), custom_call_target="tpu_custom_call" | custom-call | tf_op jit(solution)/shard_map/pallas_call | solution.py:304
  75.4 0.7 copy.11
  76.1 0.7 copy.12
  76.7 0.7 copy.13
Async XLA Ops:
  1.5 0.9 %copy-start = (bf16[256,256]{1,0:T(8,128)(2,1)S(1)}, bf16[256,256]{1,0:T(8,128)(2,1)}, u32[]{:S(2)}) copy-start(bf16[256,256]{1,0:T(8,128)(2,1)} %gate_ref.1) | copy-start | bytes 393220
  2.4 0.9 %copy-start.1 = (bf16[256,256]{1,0:T(8,128)(2,1)S(1)}, bf16[256,256]{1,0:T(8,128)(2,1)}, u32[]{:S(2)}) copy-start(bf16[256,256]{1,0:T(8,128)(2,1)} %up_ref.1) | copy-start | bytes 393220
  3.3 0.9 %copy-start.2 = (bf16[256,256]{1,0:T(8,128)(2,1)S(1)}, bf16[256,256]{1,0:T(8,128)(2,1)}, u32[]{:S(2)}) copy-start(bf16[256,256]{1,0:T(8,128)(2,1)} %down_ref.1) | copy-start | bytes 393220

commit v2 on v1

--- a/solution.py
+++ b/solution.py
@@ -15,10 +15,10 @@
 
 
 def kernel(
-    gate_ref,
-    up_ref,
-    down_ref,
-    go_ref,
+    gate_hbm,
+    up_hbm,
+    down_hbm,
+    go_hbm,
     ggrad_ref,
     ugrad_ref,
     wgrad_ref,
@@ -30,7 +30,11 @@
     ups,
     part,
     got,
+    m3,
+    m4,
     hg,
+    gate_ref,
+    up_ref,
     a1,
     b1,
     a2r,
@@ -39,11 +43,17 @@
     b2l,
     pa,
     pb,
-    wr,
-    wl,
+    w1,
+    w2,
+    w3,
+    w4,
     wp,
     hp,
     rs,
+    m3a,
+    m4a,
+    m3b,
+    m4b,
     s1,
     s2,
     sp,
@@ -52,6 +62,7 @@
     swp,
     sh,
     srs,
+    loc,
 ):
     row, col = lax.axis_index("row"), lax.axis_index("col")
     z, c = lax.div(row, 2), lax.rem(row, 2)
@@ -84,14 +95,16 @@
         pl.semaphore_signal(barrier, inc=1, device_id=at_z(md(z + k)))
     pl.semaphore_signal(barrier, inc=1, device_id=partner)
 
-    eye = (
-        lax.broadcasted_iota(jnp.int32, (64, 64), 0)
-        == lax.broadcasted_iota(jnp.int32, (64, 64), 1)
-    ).astype(BF)
-    gt[y, x] = lax.dot_general(
-        eye, go_ref[...], (((1,), (1,)), ((), ())), preferred_element_type=F32
-    ).astype(BF)
-    wf[z, c] = down_ref[...]
+    loads = [
+        pltpu.make_async_copy(go_hbm, gt.at[y, x], loc.at[0]),
+        pltpu.make_async_copy(down_hbm, wf.at[z, c], loc.at[1]),
+        pltpu.make_async_copy(gate_hbm, gate_ref, loc.at[2]),
+        pltpu.make_async_copy(up_hbm, up_ref, loc.at[3]),
+    ]
+    for load in loads:
+        load.start()
+    loads[0].wait()
+    loads[1].wait()
 
     pl.semaphore_wait(barrier, 3 * (N - 1) + 1)
 
@@ -104,24 +117,39 @@
     def w_ref(v, half=None):
         return wf.at[v, c] if half is None else wf.at[v, c, pl.ds(128 * half, 128)]
 
-    def w_step(s):
-        right = w_ref(md(z - s), 0 if s == 3 else None)
-        left = w_ref(md(z + s), 1 if s == 3 else None)
-        if s > 0:
-            full_r, full_l = w_ref(md(z - s)), w_ref(md(z + s))
-            arrived(full_r, wr.at[s - 1])
-            send(right, right, sw, wr.at[s], at_z(md(z + 1)))
-            arrived(full_l, wl.at[s - 1])
-            send(left, left, sw, wl.at[s], at_z(md(z - 1)))
-            send(full_r, full_r, swp, wp, partner)
-            send(full_l, full_l, swp, wp, partner)
-        else:
-            send(right, right, sw, wr.at[s], at_z(md(z + 1)))
-            send(left, left, sw, wl.at[s], at_z(md(z - 1)))
-            send(right, right, swp, wp, partner)
-
-    w_step(0)
-
+    def w_share(v):
+        send(w_ref(v), w_ref(v), swp, wp, partner)
+
+    def w_first():
+        mine = w_ref(z)
+        for d, way in ((0, 1), (1, -1)):
+            send(mine, mine, sw, w2.at[d], at_z(md(z + 2 * way)))
+            send(mine, mine, sw, w1.at[d], at_z(md(z + way)))
+        w_share(z)
+
+    def w_second():
+        for d, way in ((0, 1), (1, -1)):
+            near, far = md(z - way), md(z - 2 * way)
+            arrived(w_ref(far), w2.at[d])
+            send(w_ref(far), w_ref(far), sw, w3.at[d], at_z(md(z + way)))
+            send(w_ref(far, d), w_ref(far, d), sw, w4.at[d], at_z(md(z + 2 * way)))
+            arrived(w_ref(near), w1.at[d])
+            w_share(far)
+            w_share(near)
+
+    def w_last():
+        for d, way in ((0, 1), (1, -1)):
+            v = md(z - 3 * way)
+            arrived(w_ref(v), w3.at[d])
+            w_share(v)
+        for d in (0, 1):
+            arrived(w_ref(md(z + 4), d), w4.at[d])
+        w_share(md(z + 4))
+
+    w_first()
+
+    loads[2].wait()
+    loads[3].wait()
     gate = gate_ref[...].astype(F32)
     up = up_ref[...].astype(F32)
     sig = jax.nn.sigmoid(gate)
@@ -187,17 +215,29 @@
             preferred_element_type=F32,
         )
         part[yv, :, pl.ds(0, 32)] = total.astype(BF).reshape(4, 32, 256)
-        away = md(yv - z)
-
-        @pl.when(away != 0)
-        def _():
-            send(
-                part.at[yv, slice(None), pl.ds(0, 32)],
-                got.at[away - 1, slice(None), pl.ds(0, 32)],
-                srs,
-                rs,
-                at_z(yv),
-            )
+        o = md(yv - z)
+        d = lax.div(o, 4)
+        toward = at_z(md(z + 1 - 2 * d))
+        rows = part.at[yv, slice(None), pl.ds(0, 32)]
+
+        @pl.when(jnp.logical_or(o == 1, o == 7))
+        def _():
+            send(rows, got.at[d, slice(None), pl.ds(0, 32)], srs, rs, toward)
+
+        @pl.when(jnp.logical_or(o == 3, o == 5))
+        def _():
+            send(rows, m3.at[d, slice(None), pl.ds(0, 32)], srs, m3a.at[d], toward)
+
+        @pl.when(o == 4)
+        def _():
+            for e, way in ((0, 1), (1, -1)):
+                send(
+                    part.at[yv, slice(None), pl.ds(16 * e, 16)],
+                    m4.at[e, slice(None), pl.ds(0, 16)],
+                    srs,
+                    m4a.at[e],
+                    at_z(md(z + 2 * way)),
+                )
 
         @pl.when(lax.div(xv, 4) == c)
         def _():
@@ -213,54 +253,123 @@
                 preferred_element_type=F32,
             )
             part[:, xi, pl.ds(32, 32)] = total_b.astype(BF).reshape(N, 32, 256)
-            for k in (4, 3, 5, 2, 6, 1, 7):
+            for e, way in ((0, 1), (1, -1)):
                 send(
-                    part.at[md(z + k), xi, pl.ds(32, 32)],
-                    got.at[k - 1, xi, pl.ds(32, 32)],
+                    part.at[md(z + 4), xi, pl.ds(32 + 16 * e, 16)],
+                    m4.at[e, xi, pl.ds(16, 16)],
+                    srs,
+                    m4b.at[e, xi],
+                    at_z(md(z + 2 * way)),
+                )
+                send(
+                    part.at[md(z + 3 * way), xi, pl.ds(32, 32)],
+                    m3.at[e, xi, pl.ds(32, 32)],
+                    srs,
+                    m3b.at[e, xi],
+                    at_z(md(z + way)),
+                )
+            for e, way in ((0, 1), (1, -1)):
+                send(
+                    part.at[md(z + way), xi, pl.ds(32, 32)],
+                    got.at[e, xi, pl.ds(32, 32)],
                     srs,
                     rs,
-                    at_z(md(z + k)),
+                    at_z(md(z + way)),
+                )
+
+    def pass_on(yv, xv):
+        o = md(yv - z)
+
+        @pl.when(jnp.logical_or(o == 2, o == 6))
+        def _():
+            d = lax.div(o, 4)
+            arrived(m3.at[d, slice(None), pl.ds(0, 32)], m3a.at[d])
+            arrived(m4.at[d, slice(None), pl.ds(0, 16)], m4a.at[d])
+            summed = part[yv, :, pl.ds(0, 32)].astype(F32) + m3[
+                d, :, pl.ds(0, 32)
+            ].astype(F32)
+            lower = m4[d, :, pl.ds(0, 16)].astype(F32)
+            first = (d == 0).astype(F32)
+            summed = summed + jnp.concatenate(
+                [lower * first, lower * (1.0 - first)], axis=1
+            )
+            part[yv, :, pl.ds(0, 32)] = summed.astype(BF)
+            send(
+                part.at[yv, slice(None), pl.ds(0, 32)],
+                got.at[2 + d, slice(None), pl.ds(0, 32)],
+                srs,
+                rs,
+                at_z(yv),
+            )
+
+        @pl.when(lax.div(xv, 4) == c)
+        def _():
+            xi = lax.rem(xv, 4)
+            for e, way in ((0, 1), (1, -1)):
+                v = md(z + 2 * way)
+                arrived(m3.at[e, xi, pl.ds(32, 32)], m3b.at[e, xi])
+                arrived(m4.at[e, xi, pl.ds(16, 16)], m4b.at[e, xi])
+                for h in (0, 1):
+                    at = pl.ds(32 + 16 * h, 16)
+                    summed = part[v, xi, at].astype(F32) + m3[e, xi, at].astype(F32)
+                    if h == e:
+                        summed = summed + m4[e, xi, pl.ds(16, 16)].astype(F32)
+                    part[v, xi, at] = summed.astype(BF)
+                send(
+                    part.at[v, xi, pl.ds(32, 32)],
+                    got.at[2 + e, xi, pl.ds(32, 32)],
+                    srs,
+                    rs,
+                    at_z(v),
                 )
 
     for k in range(1, N):
         arrived(gt.at[y, md(x - k), pl.ds(0, 32)], a1.at[k])
         arrived(gt.at[md(y - k), x, pl.ds(32, 32)], b1.at[k])
+    spots = [(y, x)]
+    for k in (1, 2, 3):
+        spots.append((md(y - k), md(x - k)))
+        spots.append((md(y + k), md(x + k)))
+    spots.append((md(y + 4), md(x + 4)))
+
     ring(0, 0)
     ring(0, 1)
-    share(0, y, x)
+    share(0, *spots[0])
     arrived(hid.at[1], hp)
+    reduce(0, *spots[0])
     ring(1, 0)
     ring(1, 1)
-    share(1, md(y - 1), md(x - 1))
-    share(2, md(y + 1), md(x + 1))
-    reduce(0, y, x)
-    w_step(1)
+    share(1, *spots[1])
+    share(2, *spots[2])
+    w_second()
+    reduce(1, *spots[1])
+    reduce(2, *spots[2])
     ring(2, 0)
     ring(2, 1)
-    share(3, md(y - 2), md(x - 2))
-    share(4, md(y + 2), md(x + 2))
-    reduce(1, md(y - 1), md(x - 1))
-    reduce(2, md(y + 1), md(x + 1))
-    w_step(2)
+    share(3, *spots[3])
+    share(4, *spots[4])
+    reduce(3, *spots[3])
+    reduce(4, *spots[4])
     ring(3, 0)
     ring(3, 1)
-    share(5, md(y - 3), md(x - 3))
-    share(6, md(y + 3), md(x + 3))
-    reduce(3, md(y - 2), md(x - 2))
-    reduce(4, md(y + 2), md(x + 2))
-    w_step(3)
+    share(5, *spots[5])
+    share(6, *spots[6])
+    w_last()
+    reduce(5, *spots[5])
+    reduce(6, *spots[6])
     arrived(a_ref(md(y + 4), 0), a2r.at[3, 0])
     arrived(a_ref(md(y + 4), 1), a2l.at[3, 1])
     arrived(b_ref(md(x + 4), 0), b2r.at[3, 0])
     arrived(b_ref(md(x + 4), 1), b2l.at[3, 1])
-    share(7, md(y + 4), md(x + 4))
-    reduce(5, md(y - 3), md(x - 3))
-    reduce(6, md(y + 3), md(x + 3))
-    reduce(7, md(y + 4), md(x + 4))
-    far = md(z + 4)
-    arrived(w_ref(far, 0), wr.at[3])
-    arrived(w_ref(far, 1), wl.at[3])
-    send(w_ref(far), w_ref(far), swp, wp, partner)
+    share(7, *spots[7])
+    reduce(7, *spots[7])
+    pass_on(*spots[0])
+    pass_on(*spots[1])
+    pass_on(*spots[2])
+    pass_on(*spots[3])
+    pass_on(*spots[4])
+    pass_on(*spots[5])
+    pass_on(*spots[6])
     arrived(wf.at[slice(None), cp], wp)
 
     hg[...] = jnp.zeros_like(hg)
@@ -275,6 +384,7 @@
             preferred_element_type=F32,
         )
 
+    pass_on(*spots[7])
     ugrad_ref[...] = (hg[...] * act[...]).astype(BF)
     ggrad_ref[...] = (hg[...] * ups[...]).astype(BF)
 
@@ -289,22 +399,35 @@
     arrived(wf.at[slice(0, 7), 0], sw)
     arrived(wf.at[slice(None), 0], swp)
     arrived(hid.at[0], sh)
-    arrived(got, srs)
+    arrived(part.at[slice(0, 7)], srs)
     arrived(got, rs)
     total = own
-    for k in range(N - 1):
+    for k in range(4):
         total = total + got[k].reshape(256, 256).astype(F32)
     wgrad_ref[...] = (total * (1.0 / 64.0)).astype(BF)
 
 
+def store(gg_ref, ug_ref, wg_ref, gg_hbm, ug_hbm, wg_hbm, sem):
+    copies = [
+        pltpu.make_async_copy(gg_ref, gg_hbm, sem.at[0]),
+        pltpu.make_async_copy(ug_ref, ug_hbm, sem.at[1]),
+        pltpu.make_async_copy(wg_ref, wg_hbm, sem.at[2]),
+    ]
+    for copy in copies:
+        copy.start()
+    for copy in copies:
+        copy.wait()
+
+
 def per_device(gate_pre, up_pre, down_t, grad_out):
     vmem = pl.BlockSpec(memory_space=pltpu.VMEM)
+    hbm = pl.BlockSpec(memory_space=pltpu.HBM)
     block = jax.ShapeDtypeStruct((256, 256), BF)
     dma = pltpu.SemaphoreType.DMA
-    return pl.pallas_call(
+    results = pl.pallas_call(
         kernel,
         out_shape=(block, block, block),
-        in_specs=[vmem] * 4,
+        in_specs=[hbm] * 4,
         out_specs=(vmem, vmem, vmem),
         scratch_shapes=[
             pltpu.VMEM((N, N, 64, 256), BF),
@@ -314,8 +437,12 @@
             pltpu.VMEM((256, 256), F32),
             pltpu.VMEM((256, 256), F32),
             pltpu.VMEM((N, 4, 64, 256), BF),
-            pltpu.VMEM((N - 1, 4, 64, 256), BF),
+            pltpu.VMEM((4, 4, 64, 256), BF),
+            pltpu.VMEM((2, 4, 64, 256), BF),
+            pltpu.VMEM((2, 4, 32, 256), BF),
             pltpu.VMEM((256, 256), F32),
+            pltpu.VMEM((256, 256), BF),
+            pltpu.VMEM((256, 256), BF),
             dma((N,)),
             dma((N,)),
             dma((4, 2)),
@@ -324,24 +451,38 @@
             dma((4, 2)),
             dma((N,)),
             dma((N,)),
+            dma((2,)),
+            dma((2,)),
+            dma((2,)),
+            dma((2,)),
+            dma,
+            dma,
+            dma,
+            dma((2,)),
+            dma((2,)),
+            dma((2, 4)),
+            dma((2, 4)),
+            dma,
+            dma,
+            dma,
+            dma,
+            dma,
+            dma,
+            dma,
+            dma,
             dma((4,)),
-            dma((4,)),
-            dma,
-            dma,
-            dma,
-            dma,
-            dma,
-            dma,
-            dma,
-            dma,
-            dma,
-            dma,
-            dma,
         ],
         compiler_params=pltpu.CompilerParams(
-            collective_id=0, has_side_effects=True, vmem_limit_bytes=40 << 20
+            collective_id=0, has_side_effects=True
         ),
-    )(gate_pre, up_pre, down_t, grad_out)
+    )(gate_pre, up_pre, down_t, grad_out.T)
+    return pl.pallas_call(
+        store,
+        out_shape=(block, block, block),
+        in_specs=[vmem] * 3,
+        out_specs=(hbm, hbm, hbm),
+        scratch_shapes=[dma((3,))],
+    )(*results)
 
 
 def solution(mesh):

time: 77.7 us -> 58.8 us (0.76)
  the two profiles are of different devices: /device:TPU:58 before, /device:TPU:1 now
where the time goes in v2:
time: 58.8 us; the launch traced here: 58.4 us
  Pallas kernels  57.7 us (98%)
  between operations  0.64 us (1%)
    pallas_call x1, Pallas kernels, per_device(): pl.pallas_call(kernel, out_shape=(block, block, block), in_specs=[hbm] *...  55.9 us
    pallas_call x1, Pallas kernels, per_device(): pl.pallas_call(store, out_shape=(block, block, block), in_specs=[vmem] *...  1.8 us

profile of v2, /device:TPU:1, one launch (start us, length us, event | category | flops | bytes accessed | tf_op | source)
XLA Modules:
  0.0 58.4 jit_solution(10392929420413815145)
XLA Ops:
  0.6 55.9 %shard_map.67 = (bf16[256,256]{1,0:T(8,128)(2,1)}, bf16[256,256]{1,0:T(8,128)(2,1)}, bf16[256,256]{1,0:T(8,128)(2,1)}) custom-call(bf16[256,256]{1,0:T(8,128)(2,1)} %gate_hbm.1, bf16[256,256]{1,0:T(8,128)(2,1)} %up_hbm.1, bf16[256,256]{1,0:T(8,128)(2,1)} %down_hbm.1, bf16[64,256]{1,0:T(8,128)(2,1)} %bitcast.1), custom_call_target="tpu_custom_call" | custom-call | tf_op jit(solution)/shard_map/pallas_call | solution.py:427
  56.6 1.8 %shard_map.68 = (bf16[256,256]{1,0:T(8,128)(2,1)}, bf16[256,256]{1,0:T(8,128)(2,1)}, bf16[256,256]{1,0:T(8,128)(2,1)}) custom-call(bf16[256,256]{1,0:T(8,128)(2,1)} %get-tuple-element.6.gg_ref, bf16[256,256]{1,0:T(8,128)(2,1)} %get-tuple-element.7.ug_ref, bf16[256,256]{1,0:T(8,128)(2,1)} %get-tuple-element.8.wg_ref), custom_call_target="tpu_custom_call" | custom-call | tf_op jit(solution)/shard_map/pallas_call | solution.py:479

commit v3 on v2

--- a/solution.py
+++ b/solution.py
@@ -92,7 +92,8 @@
     for k in range(1, N):
         pl.semaphore_signal(barrier, inc=1, device_id=at_x(md(x + k)))
         pl.semaphore_signal(barrier, inc=1, device_id=at_y(md(y + k)))
-        pl.semaphore_signal(barrier, inc=1, device_id=at_z(md(z + k)))
+        if k in (1, 2, 6, 7):
+            pl.semaphore_signal(barrier, inc=1, device_id=at_z(md(z + k)))
     pl.semaphore_signal(barrier, inc=1, device_id=partner)
 
     loads = [
@@ -106,7 +107,7 @@
     loads[0].wait()
     loads[1].wait()
 
-    pl.semaphore_wait(barrier, 3 * (N - 1) + 1)
+    pl.semaphore_wait(barrier, 2 * (N - 1) + 5)
 
     own_a = gt.at[y, x, pl.ds(0, 32)]
     own_b = gt.at[y, x, pl.ds(32, 32)]
@@ -473,7 +474,7 @@
             dma((4,)),
         ],
         compiler_params=pltpu.CompilerParams(
-            collective_id=0, has_side_effects=True
+            collective_id=0, has_side_effects=True, vmem_limit_bytes=56130000
         ),
     )(gate_pre, up_pre, down_t, grad_out.T)
     return pl.pallas_call(
@@ -482,6 +483,7 @@
         in_specs=[vmem] * 3,
         out_specs=(hbm, hbm, hbm),
         scratch_shapes=[dma((3,))],
+        compiler_params=pltpu.CompilerParams(vmem_limit_bytes=1 << 20),
     )(*results)
 
 

time: 58.8 us -> 57.9 us (0.985)
  Pallas kernels: 57.7 us -> 56.3 us
  local copies, waits for them, and re-layouts: 0 us -> 0.75 us
    pallas_call x1, Pallas kernels: 1.8 us -> 0.77 us  [per_device(): pl.pallas_call(store, out_shape=(block, block, block), in_specs=[vmem] *...]
    unnamed x0 -> x2, local copies, waits for them, and re-layouts: none -> 0.75 us
where the time goes in v3:
time: 57.9 us; the launch traced here: 57.7 us
  Pallas kernels  56.3 us (97%)
  local copies, waits for them, and re-layouts  0.75 us (1%)
  between operations  0.65 us (1%)
    pallas_call x1, Pallas kernels, per_device(): pl.pallas_call(kernel, out_shape=(block, block, block), in_specs=[hbm] *...  55.6 us

profile of v3, /device:TPU:1, one launch (start us, length us, event | category | flops | bytes accessed | tf_op | source)
XLA Modules:
  0.0 57.7 jit_solution(7284891330315328040)
XLA Ops:
  0.6 0.0 copy-start
  0.6 0.7 %copy-done = bf16[256,64]{0,1:T(8,128)(2,1)S(1)} copy-done((bf16[256,64]{0,1:T(8,128)(2,1)S(1)}, bf16[256,64]{0,1:T(8,128)(2,1)}, u32[]{:S(2)}) %copy-start) | copy-done | bytes 32792
  1.4 55.6 %shard_map.67 = (bf16[256,256]{1,0:T(8,128)(2,1)S(1)}, bf16[256,256]{1,0:T(8,128)(2,1)S(1)}, bf16[256,256]{1,0:T(8,128)(2,1)S(1)}) custom-call(bf16[256,256]{1,0:T(8,128)(2,1)} %gate_hbm.1, bf16[256,256]{1,0:T(8,128)(2,1)} %up_hbm.1, bf16[256,256]{1,0:T(8,128)(2,1)} %down_hbm.1, bf16[64,256]{1,0:T(8,128)(2,1)S(1)} %bitcast.1), custom_call_target="tpu_custom_call" | custom-call | tf_op jit(solution)/shard_map/pallas_call | solution.py:428
  56.9 0.8 %shard_map.68 = (bf16[256,256]{1,0:T(8,128)(2,1)}, bf16[256,256]{1,0:T(8,128)(2,1)}, bf16[256,256]{1,0:T(8,128)(2,1)}) custom-call(bf16[256,256]{1,0:T(8,128)(2,1)S(1)} %get-tuple-element.6.gg_ref, bf16[256,256]{1,0:T(8,128)(2,1)S(1)} %get-tuple-element.7.ug_ref, bf16[256,256]{1,0:T(8,128)(2,1)S(1)} %get-tuple-element.8.wg_ref), custom_call_target="tpu_custom_call" | custom-call | tf_op jit(solution)/shard_map/pallas_call | solution.py:480
Async XLA Ops:
  0.6 0.8 %copy-start = (bf16[256,64]{0,1:T(8,128)(2,1)S(1)}, bf16[256,64]{0,1:T(8,128)(2,1)}, u32[]{:S(2)}) copy-start(bf16[256,64]{0,1:T(8,128)(2,1)} %param.7) | copy-start | bytes 98308

commit v4 on v3

--- a/solution.py
+++ b/solution.py
@@ -476,7 +476,12 @@
         compiler_params=pltpu.CompilerParams(
             collective_id=0, has_side_effects=True, vmem_limit_bytes=56130000
         ),
-    )(gate_pre, up_pre, down_t, grad_out.T)
+    )(
+        gate_pre,
+        up_pre,
+        down_t,
+        pltpu.with_memory_space_constraint(grad_out.T, pltpu.HBM),
+    )
     return pl.pallas_call(
         store,
         out_shape=(block, block, block),

time: 57.9 us -> 57.5 us (level)
  local copies, waits for them, and re-layouts: 0.75 us -> 0 us
    unnamed x2 -> x0, local copies, waits for them, and re-layouts: 0.75 us -> none
where the time goes in v4:
time: 57.5 us; the launch traced here: 57.3 us
  Pallas kernels  56.7 us (99%)
  between operations  0.64 us (1%)
    pallas_call x1, Pallas kernels, per_device(): pl.pallas_call(kernel, out_shape=(block, block, block), in_specs=[hbm] *...  55.9 us

profile of v4, /device:TPU:1, one launch (start us, length us, event | category | flops | bytes accessed | tf_op | source)
XLA Modules:
  0.0 57.3 jit_solution(4731586805783111283)
XLA Ops:
  0.6 55.9 %shard_map.67 = (bf16[256,256]{1,0:T(8,128)(2,1)S(1)}, bf16[256,256]{1,0:T(8,128)(2,1)S(1)}, bf16[256,256]{1,0:T(8,128)(2,1)S(1)}) custom-call(bf16[256,256]{1,0:T(8,128)(2,1)} %gate_hbm.1, bf16[256,256]{1,0:T(8,128)(2,1)} %up_hbm.1, bf16[256,256]{1,0:T(8,128)(2,1)} %down_hbm.1, bf16[64,256]{1,0:T(8,128)(2,1)} %bitcast.1), custom_call_target="tpu_custom_call" | custom-call | tf_op jit(solution)/shard_map/pallas_call | solution.py:428
  56.5 0.8 %shard_map.68 = (bf16[256,256]{1,0:T(8,128)(2,1)}, bf16[256,256]{1,0:T(8,128)(2,1)}, bf16[256,256]{1,0:T(8,128)(2,1)}) custom-call(bf16[256,256]{1,0:T(8,128)(2,1)S(1)} %get-tuple-element.6.gg_ref, bf16[256,256]{1,0:T(8,128)(2,1)S(1)} %get-tuple-element.7.ug_ref, bf16[256,256]{1,0:T(8,128)(2,1)S(1)} %get-tuple-element.8.wg_ref), custom_call_target="tpu_custom_call" | custom-call | tf_op jit(solution)/shard_map/pallas_call | solution.py:485

commit v5 on v4

--- a/solution.py
+++ b/solution.py
@@ -89,7 +89,7 @@
         pltpu.make_async_copy(ref, ref, sem).wait()
 
     barrier = pltpu.get_barrier_semaphore()
-    for k in range(1, N):
+    for k in (4, 3, 5, 2, 6, 1, 7):
         pl.semaphore_signal(barrier, inc=1, device_id=at_x(md(x + k)))
         pl.semaphore_signal(barrier, inc=1, device_id=at_y(md(y + k)))
         if k in (1, 2, 6, 7):
@@ -393,6 +393,11 @@
         gt[z, pl.ds(4 * c, 4)].reshape(256, 256), hid[0], preferred_element_type=F32
     ) + jnp.dot(gp[z].reshape(256, 256), hid[1], preferred_element_type=F32)
 
+    arrived(got, rs)
+    total = own
+    for k in range(4):
+        total = total + got[k].reshape(256, 256).astype(F32)
+    wgrad_ref[...] = (total * (1.0 / 64.0)).astype(BF)
     arrived(gt.at[slice(0, 7), slice(0, 1)], s1)
     arrived(gt.at[slice(0, 7)], s2)
     arrived(gp.at[slice(None), slice(None), pl.ds(0, 32)], sp)
@@ -401,11 +406,6 @@
     arrived(wf.at[slice(None), 0], swp)
     arrived(hid.at[0], sh)
     arrived(part.at[slice(0, 7)], srs)
-    arrived(got, rs)
-    total = own
-    for k in range(4):
-        total = total + got[k].reshape(256, 256).astype(F32)
-    wgrad_ref[...] = (total * (1.0 / 64.0)).astype(BF)
 
 
 def store(gg_ref, ug_ref, wg_ref, gg_hbm, ug_hbm, wg_hbm, sem):

time: 57.5 us -> 57.4 us (level)
  no operation moved by 1% of the time
where the time goes in v5:
time: 57.4 us; the launch traced here: 57.2 us
  Pallas kernels  56.6 us (99%)
  between operations  0.64 us (1%)
    pallas_call x1, Pallas kernels, per_device(): pl.pallas_call(kernel, out_shape=(block, block, block), in_specs=[hbm] *...  55.8 us

profile of v5, /device:TPU:1, one launch (start us, length us, event | category | flops | bytes accessed | tf_op | source)
XLA Modules:
  0.0 57.2 jit_solution(5099680360230137339)
XLA Ops:
  0.6 55.8 %shard_map.67 = (bf16[256,256]{1,0:T(8,128)(2,1)S(1)}, bf16[256,256]{1,0:T(8,128)(2,1)S(1)}, bf16[256,256]{1,0:T(8,128)(2,1)S(1)}) custom-call(bf16[256,256]{1,0:T(8,128)(2,1)} %gate_hbm.1, bf16[256,256]{1,0:T(8,128)(2,1)} %up_hbm.1, bf16[256,256]{1,0:T(8,128)(2,1)} %down_hbm.1, bf16[64,256]{1,0:T(8,128)(2,1)} %bitcast.1), custom_call_target="tpu_custom_call" | custom-call | tf_op jit(solution)/shard_map/pallas_call | solution.py:428
  56.4 0.8 %shard_map.68 = (bf16[256,256]{1,0:T(8,128)(2,1)}, bf16[256,256]{1,0:T(8,128)(2,1)}, bf16[256,256]{1,0:T(8,128)(2,1)}) custom-call(bf16[256,256]{1,0:T(8,128)(2,1)S(1)} %get-tuple-element.6.gg_ref, bf16[256,256]{1,0:T(8,128)(2,1)S(1)} %get-tuple-element.7.ug_ref, bf16[256,256]{1,0:T(8,128)(2,1)S(1)} %get-tuple-element.8.wg_ref), custom_call_target="tpu_custom_call" | custom-call | tf_op jit(solution)/shard_map/pallas_call | solution.py:485
